TPU v7x, 32 devices: a whole 2x2x4 slice. The times are simulated.
32 devices in a mesh: dp: 4 (over z), seq: 8 (over y, x, core).
Axes of the slice: x: 2, y: 2, z: 4, core: 2. Of those that a mesh axis runs over, the one named last changes fastest.
Arguments:
- frames_in: bfloat16 [4, 4096, 1024], P('dp', 'seq'), may hold values from -16 to 16
- memory_in: bfloat16 [4, 32, 1024], P('dp', 'seq'), may hold values from -6 to 6
- w_query: bfloat16 [1024, 1024], P(None, 'dp'), may hold values from -1 to 1
- w_key: bfloat16 [1024, 1024], P(None, 'dp'), may hold values from -1 to 1
- w_value: bfloat16 [1024, 1024], P(None, 'dp'), may hold values from -0.1875 to 0.1875
- lengths: int32 [4], P('dp'), may hold values from 1024 to 4096, as said below
Outputs:
- context: bfloat16 [4, 4096, 1024], P('dp', 'seq')
- memory_out: bfloat16 [4, 32, 1024], P('dp', 'seq')
Inputs may be any that keep to these rules, and one draw needn't show every extreme that they name: `lengths`: some utterance has all 4096 frames live; every utterance has at least a quarter of them.
All inputs are finite; a program needn't handle non-finite values.
Results may differ from a plain program's by a relative error of at most 0.0071.
Values may be sent and summed in bfloat16 or wider, within the bound.
No kernel may reach another device: no remote copies, remote signals or barrier semaphores. Data moves between devices by JAX's collectives and lax.ppermute only.
A program may use at most 64 MiB of HBM per device.

v0:
```python
import jax
import jax.numpy as jnp
from jax import lax
from jax.sharding import PartitionSpec as P

HEADS = 16
LEFT = 128
RIGHT = 32


def passed_along(block, axis, distance):
    devices = range(lax.axis_size(axis))
    route = [(i - distance, i) for i in devices if i - distance in devices]
    return lax.ppermute(block, axis, route)


def attend(queries, keys, values, key_live, scale):
    utt_count, n_query, feat_width = queries.shape
    n_key = keys.shape[1]
    q_heads = queries.reshape(utt_count, n_query, HEADS, -1)
    k_heads = keys.reshape(utt_count, n_key, HEADS, -1)
    v_heads = values.reshape(utt_count, n_key, HEADS, -1)
    scores = (
        jnp.einsum("bqhe,bkhe->bhqk", q_heads, k_heads, preferred_element_type=jnp.float32) * scale
    )
    scores = jnp.where(key_live[:, None, None, :], scores, -1e30)
    row_max = jnp.max(scores, axis=-1, keepdims=True)
    probs = jnp.exp(scores - row_max)
    weights = (probs / jnp.sum(probs, axis=-1, keepdims=True)).astype(jnp.bfloat16)
    mixed = jnp.einsum("bhqk,bkhe->bqhe", weights, v_heads, preferred_element_type=jnp.float32)
    return mixed.reshape(utt_count, n_query, feat_width)


def local(frames_in, memory_in, w_query, w_key, w_value, lengths):
    utt_count, row_count, feat_width = frames_in.shape
    seg_dev = memory_in.shape[1]
    seg_len = row_count // seg_dev
    key_span = LEFT + seg_len + RIGHT
    scale = float(feat_width // HEADS) ** (-0.5)
    seq_index = lax.axis_index("seq")
    row_base = seq_index * row_count
    frame_start = 0
    bank_rows = lax.all_gather(memory_in, "seq", axis=1, tiled=True)
    row_pos = row_base + jnp.arange(row_count, dtype=jnp.int32)
    live_mask = row_pos[None, :] < lengths[:, None]
    live_blocks = live_mask.reshape(utt_count, seg_dev, seg_len)
    masked_sums = jnp.einsum(
        "bnsd,bns->bnd",
        frames_in.reshape(utt_count, seg_dev, seg_len, feat_width),
        live_blocks.astype(jnp.bfloat16),
        preferred_element_type=jnp.float32,
    )
    counts = jnp.sum(live_blocks.astype(jnp.float32), axis=2)
    summary = (masked_sums / jnp.maximum(counts, 1.0)[:, :, None]).astype(jnp.bfloat16)
    n_frame = frames_in.shape[1]
    all_rows = jnp.concatenate([frames_in, summary, bank_rows], axis=1)
    n_total = all_rows.shape[1]
    flat_rows = all_rows.reshape(utt_count * n_total, feat_width)

    def project_one(piece):
        return jnp.dot(flat_rows, piece, preferred_element_type=jnp.float32).astype(jnp.bfloat16)

    q_flat = project_one(lax.all_gather(w_query, "dp", axis=1, tiled=True))
    k_flat = project_one(lax.all_gather(w_key, "dp", axis=1, tiled=True))
    v_flat = project_one(lax.all_gather(w_value, "dp", axis=1, tiled=True))
    q_all = q_flat.reshape(utt_count, n_total, feat_width)
    k_all = k_flat.reshape(utt_count, n_total, feat_width)
    v_all = v_flat.reshape(utt_count, n_total, feat_width)
    q_frames = q_all[:, frame_start : frame_start + row_count]
    q_summary = q_all[:, n_frame : n_frame + seg_dev]
    bank_keys = k_all[:, n_frame + seg_dev :]
    bank_values = v_all[:, n_frame + seg_dev :]
    k_own = k_all[:, :row_count]
    v_own = v_all[:, :row_count]
    k_before, v_before = passed_along(
        (k_own[:, row_count - LEFT :], v_own[:, row_count - LEFT :]), "seq", 1
    )
    k_after, v_after = passed_along((k_own[:, :RIGHT], v_own[:, :RIGHT]), "seq", -1)
    k_ext = jnp.concatenate([k_before, k_own, k_after], axis=1)
    v_ext = jnp.concatenate([v_before, v_own, v_after], axis=1)
    bank_count = bank_keys.shape[1]
    bank_index = jnp.arange(bank_count, dtype=jnp.int32)
    bank_ready = bank_index[None, :] * seg_len < lengths[:, None]

    def one_segment(seg_index):
        global_seg = seq_index * seg_dev + seg_index
        q_rows = lax.dynamic_slice_in_dim(q_frames, seg_index * seg_len, seg_len, 1)
        q_sum = lax.dynamic_slice_in_dim(q_summary, seg_index, 1, 1)
        queries = jnp.concatenate([q_rows, q_sum], axis=1)
        k_window = lax.dynamic_slice_in_dim(k_ext, seg_index * seg_len, key_span, 1)
        v_window = lax.dynamic_slice_in_dim(v_ext, seg_index * seg_len, key_span, 1)
        frame_pos = row_base - LEFT + seg_index * seg_len + jnp.arange(key_span, dtype=jnp.int32)
        frame_live = (frame_pos[None, :] >= 0) & (frame_pos[None, :] < lengths[:, None])
        key_live = jnp.concatenate(
            [bank_ready & (bank_index < global_seg)[None, :], frame_live], axis=1
        )
        keys = jnp.concatenate([bank_keys, k_window], axis=1)
        values = jnp.concatenate([bank_values, v_window], axis=1)
        return attend(queries, keys, values, key_live, scale)

    attended = lax.map(one_segment, jnp.arange(seg_dev, dtype=jnp.int32))
    frame_part = (
        attended[:, :, :seg_len].transpose(1, 0, 2, 3).reshape(utt_count, row_count, feat_width)
    )
    context = (frame_part * live_mask[:, :, None].astype(jnp.float32)).astype(jnp.bfloat16)
    memory_out = attended[:, :, seg_len].transpose(1, 0, 2).astype(jnp.bfloat16)
    return (context, memory_out)


def solution(mesh):
    placed = (
        P("dp", "seq", None),
        P("dp", "seq", None),
        P(None, "dp"),
        P(None, "dp"),
        P(None, "dp"),
        P("dp"),
    )
    return jax.shard_map(
        local,
        mesh=mesh,
        in_specs=placed,
        out_specs=(P("dp", "seq", None), P("dp", "seq", None)),
        check_vma=False,
    )
```

profile of v0, /device:TPU:3, one launch (start us, length us, event | category | flops | bytes accessed | tf_op | source)
XLA Modules:
  0.0 252.9 jit_solution(9510433819351743117)
XLA Ops:
  10.8 9.7 %all_gather.12 = bf16[1,32,1024]{2,0,1:T(2,128)(2,1)S(1)} all-gather(bf16[1,4,1024]{2,0,1:T(2,128)(2,1)S(1)} %copy.26), channel_id=1, replica_groups=mesh['dp'=4,'seq'=8] {'seq'}, dimensions={1}, use_global_device_ids=true | all-gather | bytes 73728 | tf_op jit(solution)/shard_map/all_gather | solution.py:43
  20.7 1.5 fusion.21
  22.3 34.8 %all-gather.4.cloned.1.call-done = bf16[1024,1024]{1,0:T(8,128)(2,1)} async-done(((bf16[1024,256]{1,0:T(8,128)(2,1)}), bf16[1024,1024]{1,0:T(8,128)(2,1)}) %all-gather.4.cloned.1.call-update) | async-done | bytes 2097168 | tf_op jit(solution)/shard_map/all_gather | solution.py:65
  57.1 2.9 %fusion.15 = bf16[1,548,1024]{2,1,0:T(8,128)(2,1)S(1)} fusion(bf16[1024,1024]{1,0:T(8,128)(2,1)} %all-gather.4.cloned.1.call-done, bf16[1,32,1024]{2,1,0:T(8,128)(2,1)S(1)} %copy.27, bf16[1,4,1024]{2,1,0:T(4,128)(2,1)S(1)} %fusion.20, bf16[1,512,1024]{2,1,0:T(8,128)(2,1)S(1)} %copy-done.3), kind=kOutput, calls=%fused_computation.30 | convolution fusion | flops 1153167360 | bytes 4341760 | tf_op jit(solution)/shard_map/dot_general | solution.py:61
  61.4 2.5 collective-permute-start.1
  64.0 3.9 %collective-permute-start = (bf16[1,128,1024]{2,1,0:T(8,128)(2,1)}, bf16[1,128,1024]{2,1,0:T(8,128)(2,1)}, u32[]{:S(2)}, u32[]{:S(2)}) collective-permute-start(bf16[1,128,1024]{2,1,0:T(8,128)(2,1)} %slice.53), channel_id=1, source_target_pairs={{0,1},{1,2},{2,3},{3,4},{4,5},{5,6},{6,7},{8,9},{9,10},{10,11},{11... | collective-permute-start | bytes 786440 | tf_op jit(solution)/shard_map/ppermute | solution.py:14
  67.9 35.3 %all-gather.8.cloned.1.call-done = bf16[1024,1024]{1,0:T(8,128)(2,1)} async-done(((bf16[1024,256]{1,0:T(8,128)(2,1)}), bf16[1024,1024]{1,0:T(8,128)(2,1)}) %all-gather.8.cloned.1.call-update) | async-done | bytes 2097168 | tf_op jit(solution)/shard_map/all_gather | solution.py:64
  103.1 2.9 %fusion.17 = bf16[1,548,1024]{2,1,0:T(8,128)(2,1)S(1)} fusion(bf16[1024,1024]{1,0:T(8,128)(2,1)} %all-gather.8.cloned.1.call-done, bf16[1,32,1024]{2,1,0:T(8,128)(2,1)S(1)} %copy.27, bf16[1,4,1024]{2,1,0:T(4,128)(2,1)S(1)} %fusion.20, bf16[1,512,1024]{2,1,0:T(8,128)(2,1)S(1)} %copy-done.3), kind=kOutput, calls=%fused_computation.32 | convolution fusion | flops 1153167360 | bytes 4341760 | tf_op jit(solution)/shard_map/dot_general | solution.py:61
  106.9 3.6 %collective-permute-start.2 = (bf16[1,128,1024]{2,1,0:T(8,128)(2,1)}, bf16[1,128,1024]{2,1,0:T(8,128)(2,1)}, u32[]{:S(2)}, u32[]{:S(2)}) collective-permute-start(bf16[1,128,1024]{2,1,0:T(8,128)(2,1)} %slice.59), channel_id=1, source_target_pairs={{0,1},{1,2},{2,3},{3,4},{4,5},{5,6},{6,7},{8,9},{9,10},{10,11},{11... | collective-permute-start | bytes 786440 | tf_op jit(solution)/shard_map/ppermute | solution.py:14
  110.5 38.7 %all-gather.6.cloned.1.call-done = bf16[1024,1024]{1,0:T(8,128)(2,1)} async-done(((bf16[1024,256]{1,0:T(8,128)(2,1)}), bf16[1024,1024]{1,0:T(8,128)(2,1)}) %all-gather.6.cloned.1.call-update) | async-done | bytes 2097168 | tf_op jit(solution)/shard_map/all_gather | solution.py:63
  149.2 2.9 %fusion.16 = bf16[1,548,1024]{2,1,0:T(8,128)(2,1)S(1)} fusion(bf16[1024,1024]{1,0:T(8,128)(2,1)} %all-gather.6.cloned.1.call-done, bf16[1,32,1024]{2,1,0:T(8,128)(2,1)S(1)} %copy.27, bf16[1,4,1024]{2,1,0:T(4,128)(2,1)S(1)} %fusion.20, bf16[1,512,1024]{2,1,0:T(8,128)(2,1)S(1)} %copy-done.3), kind=kOutput, calls=%fused_computation.31 | convolution fusion | flops 1153167360 | bytes 4341760 | tf_op jit(solution)/shard_map/dot_general | solution.py:61
  154.2 2.7 %collective-permute-start.3 = (bf16[1,32,1024]{2,1,0:T(8,128)(2,1)S(1)}, bf16[1,32,1024]{2,1,0:T(8,128)(2,1)S(1)}, u32[]{:S(2)}, u32[]{:S(2)}) collective-permute-start(bf16[1,32,1024]{2,1,0:T(8,128)(2,1)S(1)} %get-tuple-element.266), channel_id=1, source_target_pairs={{1,0},{2,1},{3,2},{4,3},{5,4},{6,5},{7,6},{9,8},{10,9},{11,10},{12... | collective-permute-start | bytes 196616 | tf_op jit(solution)/shard_map/ppermute | solution.py:14
  157.9 1.4 pad_maximum_fusion.3
  159.3 1.5 collective-permute-done.3
  160.9 2.2 pad_maximum_fusion.4
  163.1 72.8 %while.13 = (s32[]{:T(128)}, f32[4,1,129,1024]{2,3,1,0:T(8,128)}, s32[4]{0:T(128)S(1)}, bf16[1,672,1024]{2,1,0:T(8,128)(2,1)S(1)}, bf16[1,32,1024]{1,2,0:T(8,128...) while((s32[]{:T(128)}, f32[4,1,129,1024]{2,3,1,0:T(8,128)}, ...), condition=%wide.region_4.5_spmd.clone, body=%wide.region_1.4_spmd.clone.sunk | while | flops 176197520 | bytes 28918032 | solution.py:101
  166.3 1.8 pad_maximum_fusion.7
  173.7 3.0 %fusion.45 = (f32[16,129]{1,0:T(8,128)S(1)}, f32[16,129,320]{2,1,0:T(8,128)}) fusion(pred[320]{0:T(512)(128)(4,1)S(1)} %add_reduce_fusion.2, bf16[129,16,64]{0,2,1:T(8,128)(2,1)S(1)} %bitcast.76, bf16[320,16,64]{0,2,1:T(8,128)(2,1)S(1)} %bitcast.75), kind=kOutput, calls=%fused_computation.50.clone.1 | convolution fusion | flops 87183680 | bytes 3570048 | tf_op jit(solution)/shard_map/while/body/eval_jaxpr/sub | solution.py:28
  176.7 2.9 %fusion.46 = f32[16,64,129]{2,1,0:T(8,128)S(1)} fusion(bf16[320,16,64]{0,2,1:T(8,128)(2,1)S(1)} %bitcast.74, f32[16,129,320]{2,1,0:T(8,128)} %get-tuple-element.354, f32[16,129]{1,0:T(8,128)S(1)} %get-tuple-element.355), kind=kOutput, calls=%fused_computation.9.clone.1 | convolution fusion | flops 85862400 | bytes 3833920 | tf_op jit(solution)/shard_map/while/body/eval_jaxpr/bhqk,bkhe->bqhe/dot_general | solution.py:30
  184.6 1.8 pad_maximum_fusion.7
  191.9 3.0 %fusion.45 = (f32[16,129]{1,0:T(8,128)S(1)}, f32[16,129,320]{2,1,0:T(8,128)}) fusion(pred[320]{0:T(512)(128)(4,1)S(1)} %add_reduce_fusion.2, bf16[129,16,64]{0,2,1:T(8,128)(2,1)S(1)} %bitcast.76, bf16[320,16,64]{0,2,1:T(8,128)(2,1)S(1)} %bitcast.75), kind=kOutput, calls=%fused_computation.50.clone.1 | convolution fusion | flops 87183680 | bytes 3570048 | tf_op jit(solution)/shard_map/while/body/eval_jaxpr/sub | solution.py:28
  194.9 2.9 %fusion.46 = f32[16,64,129]{2,1,0:T(8,128)S(1)} fusion(bf16[320,16,64]{0,2,1:T(8,128)(2,1)S(1)} %bitcast.74, f32[16,129,320]{2,1,0:T(8,128)} %get-tuple-element.354, f32[16,129]{1,0:T(8,128)S(1)} %get-tuple-element.355), kind=kOutput, calls=%fused_computation.9.clone.1 | convolution fusion | flops 85862400 | bytes 3833920 | tf_op jit(solution)/shard_map/while/body/eval_jaxpr/bhqk,bkhe->bqhe/dot_general | solution.py:30
  202.8 1.8 pad_maximum_fusion.7
  210.1 3.0 %fusion.45 = (f32[16,129]{1,0:T(8,128)S(1)}, f32[16,129,320]{2,1,0:T(8,128)}) fusion(pred[320]{0:T(512)(128)(4,1)S(1)} %add_reduce_fusion.2, bf16[129,16,64]{0,2,1:T(8,128)(2,1)S(1)} %bitcast.76, bf16[320,16,64]{0,2,1:T(8,128)(2,1)S(1)} %bitcast.75), kind=kOutput, calls=%fused_computation.50.clone.1 | convolution fusion | flops 87183680 | bytes 3570048 | tf_op jit(solution)/shard_map/while/body/eval_jaxpr/sub | solution.py:28
  213.1 2.9 %fusion.46 = f32[16,64,129]{2,1,0:T(8,128)S(1)} fusion(bf16[320,16,64]{0,2,1:T(8,128)(2,1)S(1)} %bitcast.74, f32[16,129,320]{2,1,0:T(8,128)} %get-tuple-element.354, f32[16,129]{1,0:T(8,128)S(1)} %get-tuple-element.355), kind=kOutput, calls=%fused_computation.9.clone.1 | convolution fusion | flops 85862400 | bytes 3833920 | tf_op jit(solution)/shard_map/while/body/eval_jaxpr/bhqk,bkhe->bqhe/dot_general | solution.py:30
  221.0 1.8 pad_maximum_fusion.7
  228.3 3.0 %fusion.45 = (f32[16,129]{1,0:T(8,128)S(1)}, f32[16,129,320]{2,1,0:T(8,128)}) fusion(pred[320]{0:T(512)(128)(4,1)S(1)} %add_reduce_fusion.2, bf16[129,16,64]{0,2,1:T(8,128)(2,1)S(1)} %bitcast.76, bf16[320,16,64]{0,2,1:T(8,128)(2,1)S(1)} %bitcast.75), kind=kOutput, calls=%fused_computation.50.clone.1 | convolution fusion | flops 87183680 | bytes 3570048 | tf_op jit(solution)/shard_map/while/body/eval_jaxpr/sub | solution.py:28
  231.3 2.9 %fusion.46 = f32[16,64,129]{2,1,0:T(8,128)S(1)} fusion(bf16[320,16,64]{0,2,1:T(8,128)(2,1)S(1)} %bitcast.74, f32[16,129,320]{2,1,0:T(8,128)} %get-tuple-element.354, f32[16,129]{1,0:T(8,128)S(1)} %get-tuple-element.355), kind=kOutput, calls=%fused_computation.9.clone.1 | convolution fusion | flops 85862400 | bytes 3833920 | tf_op jit(solution)/shard_map/while/body/eval_jaxpr/bhqk,bkhe->bqhe/dot_general | solution.py:30
  235.9 3.0 %slice.51 = f32[4,1,128,1024]{2,3,1,0:T(8,128)} slice(f32[4,1,129,1024]{2,3,1,0:T(8,128)} %get-tuple-element.165), slice={[0:4], [0:1], [0:128], [0:1024]} | slice | bytes 4194304 | tf_op jit(solution)/shard_map/slice | solution.py:103
  239.0 3.7 %copy.35 = bf16[4,1,129,1024]{3,0,2,1:T(4,128)(2,1)S(1)} copy(f32[4,1,129,1024]{2,3,1,0:T(8,128)} %get-tuple-element.165) | data formatting | bytes 3170304 | tf_op jit(solution)/shard_map/while | solution.py:101
  242.7 1.9 copy.34
  245.2 1.1 fusion.14
  (106 shorter events, 37.5 us)
Async XLA Ops:
  7.2 49.9 %copy-start.3 = (bf16[1,512,1024]{2,1,0:T(8,128)(2,1)S(1)}, bf16[1,512,1024]{2,1,0:T(8,128)(2,1)}, u32[]{:S(2)}) copy-start(bf16[1,512,1024]{2,1,0:T(8,128)(2,1)} %param.8) | copy-start | bytes 3145732
  7.2 49.9 %all-gather.4.cloned.1.call-start = ((), (), s32[]{:S(2)}) async-start(), calls=%async_computation | async-start | bytes 2621440 | tf_op jit(solution)/shard_map/all_gather | solution.py:65
  7.9 95.2 %all-gather.8.cloned.1.call-start = ((), (), s32[]{:S(2)}) async-start(), calls=%async_computation.2 | async-start | bytes 2621440 | tf_op jit(solution)/shard_map/all_gather | solution.py:64
  8.7 140.5 %all-gather.6.cloned.1.call-start = ((), (), s32[]{:S(2)}) async-start(), calls=%async_computation.1 | async-start | bytes 2621440 | tf_op jit(solution)/shard_map/all_gather | solution.py:63
  61.4 96.5 %collective-permute-start.1 = (bf16[1,32,1024]{2,1,0:T(8,128)(2,1)}, bf16[1,32,1024]{2,1,0:T(8,128)(2,1)S(1)}, u32[]{:S(2)}, u32[]{:S(2)}) collective-permute-start(bf16[1,32,1024]{2,1,0:T(8,128)(2,1)} %get-tuple-element.268), channel_id=1, source_target_pairs={{1,0},{2,1},{3,2},{4,3},{5,4},{6,5},{7,6},{9,8},{10,9},{11,10},{12... | collective-permute-start | bytes 196616 | tf_op jit(solution)/shard_map/ppermute | solution.py:14
  64.0 94.0 %collective-permute-start = (bf16[1,128,1024]{2,1,0:T(8,128)(2,1)}, bf16[1,128,1024]{2,1,0:T(8,128)(2,1)}, u32[]{:S(2)}, u32[]{:S(2)}) collective-permute-start(bf16[1,128,1024]{2,1,0:T(8,128)(2,1)} %slice.53), channel_id=1, source_target_pairs={{0,1},{1,2},{2,3},{3,4},{4,5},{5,6},{6,7},{8,9},{9,10},{10,11},{11... | collective-permute-start | bytes 786440 | tf_op jit(solution)/shard_map/ppermute | solution.py:14
  106.1 47.1 %copy-start.2 = (bf16[1,548,1024]{2,1,0:T(8,128)(2,1)}, bf16[1,548,1024]{2,1,0:T(8,128)(2,1)S(1)}, u32[]{:S(2)}) copy-start(bf16[1,548,1024]{2,1,0:T(8,128)(2,1)S(1)} %fusion.17) | copy-start | bytes 3366916
  106.9 54.0 %collective-permute-start.2 = (bf16[1,128,1024]{2,1,0:T(8,128)(2,1)}, bf16[1,128,1024]{2,1,0:T(8,128)(2,1)}, u32[]{:S(2)}, u32[]{:S(2)}) collective-permute-start(bf16[1,128,1024]{2,1,0:T(8,128)(2,1)} %slice.59), channel_id=1, source_target_pairs={{0,1},{1,2},{2,3},{3,4},{4,5},{5,6},{6,7},{8,9},{9,10},{10,11},{11... | collective-permute-start | bytes 786440 | tf_op jit(solution)/shard_map/ppermute | solution.py:14
  154.2 6.6 %slice-start = ((bf16[1,548,1024]{2,1,0:T(8,128)(2,1)}), bf16[1,512,1024]{2,1,0:T(8,128)(2,1)S(1)}, s32[]{:S(2)}) async-start(bf16[1,548,1024]{2,1,0:T(8,128)(2,1)} %copy-done.2), calls=%async_computation.3 | async-start | bytes 2097152 | tf_op jit(solution)/shard_map/slice | solution.py:73
  154.2 6.6 %collective-permute-start.3 = (bf16[1,32,1024]{2,1,0:T(8,128)(2,1)S(1)}, bf16[1,32,1024]{2,1,0:T(8,128)(2,1)S(1)}, u32[]{:S(2)}, u32[]{:S(2)}) collective-permute-start(bf16[1,32,1024]{2,1,0:T(8,128)(2,1)S(1)} %get-tuple-element.266), channel_id=1, source_target_pairs={{1,0},{2,1},{3,2},{4,3},{5,4},{6,5},{7,6},{9,8},{10,9},{11,10},{12... | collective-permute-start | bytes 196616 | tf_op jit(solution)/shard_map/ppermute | solution.py:14
  163.1 1.8 copy-start
  179.6 1.7 copy-start.1
  181.3 1.8 copy-start
  197.8 1.7 copy-start.1
  199.5 1.8 copy-start
  216.0 1.7 copy-start.1
  217.7 1.8 copy-start
  234.2 1.7 copy-start.1
Sparse Core Ops, SparseCore 0:
  9.5 47.5 all-gather.3
  58.7 44.4 all-gather.7
  104.7 44.4 all-gather.5
where the time goes:
time: 254 us; the launch traced here: 253 us
  waiting for transfers between devices  112 us (44%)
  local copies, waits for them, and re-layouts  37.7 us (15%)
  matrix products  33.9 us (13%)
  other arithmetic  18.3 us (7%)
  between operations  14.5 us (6%)
  loops' own time  13.5 us (5%)
  starting transfers between devices  12.8 us (5%)
  blocking collectives  9.73 us (4%)
    all_gather x1, waiting for transfers between devices, local(): q_flat = project_one(lax.all_gather(w_query, 'dp', axis=1, tiled=True))  38.7 us
    all_gather x1, waiting for transfers between devices, local(): k_flat = project_one(lax.all_gather(w_key, 'dp', axis=1, tiled=True))  35.3 us
    all_gather x1, waiting for transfers between devices, local(): v_flat = project_one(lax.all_gather(w_value, 'dp', axis=1, tiled=True))  34.8 us
    another operation x1, loops' own time, local(): attended = lax.map(one_segment, jnp.arange(seg_dev, dtype=jnp.int32))  13.5 us
    ppermute x4, starting transfers between devices, passed_along(): return lax.ppermute(block, axis, route)  12.7 us
    sub x4, matrix products, attend(): probs = jnp.exp(scores - row_max)  12.1 us
    dot_general x4, matrix products, attend(): jnp.einsum('bhqk,bkhe->bqhe', weights, v_heads, preferred_element_type=jn...  11.6 us
    all_gather x1, blocking collectives, local(): bank_rows = lax.all_gather(memory_in, 'seq', axis=1, tiled=True)  9.73 us
  transfers between devices with their start and end apart: 7, of which 4 were waited for; matrix products, arithmetic and copies ran while one was open for 7% of the time, Pallas kernels for 0%

commit v1 on v0

--- a/solution.py
+++ b/solution.py
@@ -6,6 +6,11 @@
 HEADS = 16
 LEFT = 128
 RIGHT = 32
+
+
+def gather_from_all(shard, axis, dim):
+    copies = jnp.concatenate([shard] * lax.axis_size(axis), axis=dim)
+    return lax.all_to_all(copies, axis, dim, dim, tiled=True)
 
 
 def passed_along(block, axis, distance):
@@ -60,7 +65,7 @@
     def project_one(piece):
         return jnp.dot(flat_rows, piece, preferred_element_type=jnp.float32).astype(jnp.bfloat16)
 
-    q_flat = project_one(lax.all_gather(w_query, "dp", axis=1, tiled=True))
+    q_flat = project_one(gather_from_all(w_query, "dp", 1))
     k_flat = project_one(lax.all_gather(w_key, "dp", axis=1, tiled=True))
     v_flat = project_one(lax.all_gather(w_value, "dp", axis=1, tiled=True))
     q_all = q_flat.reshape(utt_count, n_total, feat_width)

time: 254 us -> 264 us (1.039)
  local copies, waits for them, and re-layouts: 37.7 us -> 45 us
  starting transfers between devices: 12.8 us -> 16.9 us
  waiting for transfers between devices: 112 us -> 109 us
    all_gather x1 -> x0, waiting for transfers between devices: 38.7 us -> none  [local(): q_flat = project_one(lax.all_gather(w_query, 'dp', axis=1, tiled=True))]
    all_gather x1, waiting for transfers between devices: 34.8 us -> 66.2 us  [local(): v_flat = project_one(lax.all_gather(w_value, 'dp', axis=1, tiled=True))]
    all_to_all x0 -> x2, local copies, waits for them, and re-layouts: none -> 5.17 us  [gather_from_all(): return lax.all_to_all(copies, axis, dim, dim, tiled=True)]
    all_to_all x0 -> x1, starting transfers between devices: none -> 4.72 us  [gather_from_all(): return lax.all_to_all(copies, axis, dim, dim, tiled=True)]
    all_gather x1, waiting for transfers between devices: 35.3 us -> 39.6 us  [local(): k_flat = project_one(lax.all_gather(w_key, 'dp', axis=1, tiled=True))]
  transfers between devices with their start and end apart: 7 -> 7, of which waited for: 4 -> 3; matrix products, arithmetic and copies ran while one was open for 7% -> 9% of each run, Pallas kernels for 0% -> 0%
where the time goes in v1:
time: 264 us; the launch traced here: 262 us
  waiting for transfers between devices  109 us (41%)
  local copies, waits for them, and re-layouts  45 us (17%)
  matrix products  33.5 us (13%)
  other arithmetic  19.1 us (7%)
  starting transfers between devices  16.9 us (6%)
  between operations  14.9 us (6%)
  loops' own time  13.4 us (5%)
  blocking collectives  10 us (4%)
    all_gather x1, waiting for transfers between devices, local(): v_flat = project_one(lax.all_gather(w_value, 'dp', axis=1, tiled=True))  66.2 us
    all_gather x1, waiting for transfers between devices, local(): k_flat = project_one(lax.all_gather(w_key, 'dp', axis=1, tiled=True))  39.6 us
    another operation x1, loops' own time, local(): attended = lax.map(one_segment, jnp.arange(seg_dev, dtype=jnp.int32))  13.4 us
    ppermute x4, starting transfers between devices, passed_along(): return lax.ppermute(block, axis, route)  12.1 us
    sub x4, matrix products, attend(): probs = jnp.exp(scores - row_max)  12 us
    dot_general x4, matrix products, attend(): jnp.einsum('bhqk,bkhe->bqhe', weights, v_heads, preferred_element_type=jn...  11.6 us
    all_gather x1, blocking collectives, local(): bank_rows = lax.all_gather(memory_in, 'seq', axis=1, tiled=True)  10 us
    dot_general x3, matrix products, project_one(): jnp.dot(flat_rows, piece, preferred_element_type=jnp.float32)  9.65 us
  transfers between devices with their start and end apart: 7, of which 3 were waited for; matrix products, arithmetic and copies ran while one was open for 9% of the time, Pallas kernels for 0%

profile of v1, /device:TPU:3, one launch (start us, length us, event | category | flops | bytes accessed | tf_op | source)
XLA Modules:
  0.0 262.3 jit_solution(12377242104426659337)
XLA Ops:
  10.2 2.6 %copy.48 = bf16[1024,4,256]{2,0,1:T(8,128)(2,1)} copy(bf16[1024,4,256]{0,2,1:T(8,128)(2,1)S(1)} %bitcast.79) | data formatting | bytes 4194304 | tf_op jit(solution)/shard_map/all_to_all | solution.py:13
  12.8 4.7 %all-to-all-start = ((bf16[1024,4,256]{2,0,1:T(8,128)(2,1)}), bf16[1024,4,256]{2,0,1:T(8,128)(2,1)S(1)}, u32[]{:S(2)}, u32[]{:S(2)}) async-start(bf16[1024,4,256]{2,0,1:T(8,128)(2,1)} %copy.48), calls=%async_computation | async-start | bytes 4194304 | tf_op jit(solution)/shard_map/all_to_all | solution.py:13
  18.2 10.0 %all_gather.9 = bf16[1,32,1024]{2,0,1:T(2,128)(2,1)S(1)} all-gather(bf16[1,4,1024]{2,0,1:T(2,128)(2,1)S(1)} %copy.42), channel_id=1, replica_groups=mesh['dp'=4,'seq'=8] {'seq'}, dimensions={1}, use_global_device_ids=true | all-gather | bytes 73728 | tf_op jit(solution)/shard_map/all_gather | solution.py:48
  29.3 66.2 %all-gather.3.cloned.1.call-done = bf16[1024,1024]{1,0:T(8,128)(2,1)} async-done(((bf16[1024,256]{1,0:T(8,128)(2,1)}), bf16[1024,1024]{1,0:T(8,128)(2,1)}) %all-gather.3.cloned.1.call-update) | async-done | bytes 2097168 | tf_op jit(solution)/shard_map/all_gather | solution.py:70
  95.5 2.9 %fusion.15 = bf16[1,548,1024]{2,1,0:T(8,128)(2,1)S(1)} fusion(bf16[1024,1024]{1,0:T(8,128)(2,1)} %all-gather.3.cloned.1.call-done, bf16[1,32,1024]{2,1,0:T(8,128)(2,1)S(1)} %copy.43, bf16[1,4,1024]{2,1,0:T(4,128)(2,1)S(1)} %fusion.20, bf16[1,512,1024]{2,1,0:T(8,128)(2,1)S(1)} %copy-done.5), kind=kOutput, calls=%fused_computation.31 | convolution fusion | flops 1153167360 | bytes 4341760 | tf_op jit(solution)/shard_map/dot_general | solution.py:66
  100.2 2.4 collective-permute-start.1
  102.6 4.1 %collective-permute-start = (bf16[1,128,1024]{2,1,0:T(8,128)(2,1)S(1)}, bf16[1,128,1024]{2,1,0:T(8,128)(2,1)}, u32[]{:S(2)}, u32[]{:S(2)}) collective-permute-start(bf16[1,128,1024]{2,1,0:T(8,128)(2,1)S(1)} %slice.53), channel_id=1, source_target_pairs={{0,1},{1,2},{2,3},{3,4},{4,5},{5,6},{6,7},{8,9},{9,10},{10,11},{11... | collective-permute-start | bytes 786440 | tf_op jit(solution)/shard_map/ppermute | solution.py:19
  106.6 39.6 %all-gather.5.cloned.1.call-done = bf16[1024,1024]{1,0:T(8,128)(2,1)} async-done(((bf16[1024,256]{1,0:T(8,128)(2,1)}), bf16[1024,1024]{1,0:T(8,128)(2,1)}) %all-gather.5.cloned.1.call-update) | async-done | bytes 2097168 | tf_op jit(solution)/shard_map/all_gather | solution.py:69
  146.3 3.3 %fusion.17 = bf16[1,548,1024]{2,1,0:T(8,128)(2,1)S(1)} fusion(bf16[1024,1024]{1,0:T(8,128)(2,1)} %all-gather.5.cloned.1.call-done, bf16[1,32,1024]{2,1,0:T(8,128)(2,1)} %copy-done.7, bf16[1,4,1024]{2,1,0:T(4,128)(2,1)} %copy-done.9, bf16[1,512,1024]{2,1,0:T(8,128)(2,1)} %param.8), kind=kOutput, calls=%fused_computation.33 | convolution fusion | flops 1153167360 | bytes 4341760 | tf_op jit(solution)/shard_map/dot_general | solution.py:66
  150.3 3.6 %collective-permute-start.2 = (bf16[1,128,1024]{2,1,0:T(8,128)(2,1)}, bf16[1,128,1024]{2,1,0:T(8,128)(2,1)}, u32[]{:S(2)}, u32[]{:S(2)}) collective-permute-start(bf16[1,128,1024]{2,1,0:T(8,128)(2,1)} %slice.59), channel_id=1, source_target_pairs={{0,1},{1,2},{2,3},{3,4},{4,5},{5,6},{6,7},{8,9},{9,10},{10,11},{11... | collective-permute-start | bytes 786440 | tf_op jit(solution)/shard_map/ppermute | solution.py:19
  154.0 2.5 copy.49
  156.5 3.4 %fusion.16 = bf16[1,548,1024]{2,1,0:T(8,128)(2,1)S(1)} fusion(bf16[1024,1024]{0,1:T(8,128)(2,1)} %bitcast.80, bf16[1,32,1024]{2,1,0:T(8,128)(2,1)} %copy-done.7, bf16[1,4,1024]{2,1,0:T(4,128)(2,1)} %copy-done.9, bf16[1,512,1024]{2,1,0:T(8,128)(2,1)} %param.8), kind=kOutput, calls=%fused_computation.32 | convolution fusion | flops 1153167360 | bytes 4341760 | tf_op jit(solution)/shard_map/dot_general | solution.py:66
  163.2 2.1 collective-permute-start.3
  166.4 1.4 pad_maximum_fusion.4
  167.8 2.1 collective-permute-done.3
  169.9 2.2 pad_maximum_fusion.5
  172.1 72.8 %while.13 = (s32[]{:T(128)}, f32[4,1,129,1024]{2,3,1,0:T(8,128)}, s32[4]{0:T(128)S(1)}, bf16[1,672,1024]{2,1,0:T(8,128)(2,1)S(1)}, bf16[1,32,1024]{1,2,0:T(8,128...) while((s32[]{:T(128)}, f32[4,1,129,1024]{2,3,1,0:T(8,128)}, ...), condition=%wide.region_4.5_spmd.clone, body=%wide.region_1.4_spmd.clone.sunk | while | flops 176197520 | bytes 28918032 | solution.py:106
  175.4 1.8 pad_maximum_fusion.8
  182.7 3.0 %fusion.45 = (f32[16,129]{1,0:T(8,128)S(1)}, f32[16,129,320]{2,1,0:T(8,128)}) fusion(pred[320]{0:T(512)(128)(4,1)S(1)} %add_reduce_fusion.2, bf16[129,16,64]{0,2,1:T(8,128)(2,1)S(1)} %bitcast.78, bf16[320,16,64]{0,2,1:T(8,128)(2,1)S(1)} %bitcast.77), kind=kOutput, calls=%fused_computation.51.clone.1 | convolution fusion | flops 87183680 | bytes 3570048 | tf_op jit(solution)/shard_map/while/body/eval_jaxpr/sub | solution.py:33
  185.7 2.9 %fusion.46 = f32[16,64,129]{2,1,0:T(8,128)S(1)} fusion(bf16[320,16,64]{0,2,1:T(8,128)(2,1)S(1)} %bitcast.76, f32[16,129,320]{2,1,0:T(8,128)} %get-tuple-element.367, f32[16,129]{1,0:T(8,128)S(1)} %get-tuple-element.368), kind=kOutput, calls=%fused_computation.9.clone.1 | convolution fusion | flops 85862400 | bytes 3833920 | tf_op jit(solution)/shard_map/while/body/eval_jaxpr/bhqk,bkhe->bqhe/dot_general | solution.py:35
  193.6 1.8 pad_maximum_fusion.8
  200.9 3.0 %fusion.45 = (f32[16,129]{1,0:T(8,128)S(1)}, f32[16,129,320]{2,1,0:T(8,128)}) fusion(pred[320]{0:T(512)(128)(4,1)S(1)} %add_reduce_fusion.2, bf16[129,16,64]{0,2,1:T(8,128)(2,1)S(1)} %bitcast.78, bf16[320,16,64]{0,2,1:T(8,128)(2,1)S(1)} %bitcast.77), kind=kOutput, calls=%fused_computation.51.clone.1 | convolution fusion | flops 87183680 | bytes 3570048 | tf_op jit(solution)/shard_map/while/body/eval_jaxpr/sub | solution.py:33
  203.9 2.9 %fusion.46 = f32[16,64,129]{2,1,0:T(8,128)S(1)} fusion(bf16[320,16,64]{0,2,1:T(8,128)(2,1)S(1)} %bitcast.76, f32[16,129,320]{2,1,0:T(8,128)} %get-tuple-element.367, f32[16,129]{1,0:T(8,128)S(1)} %get-tuple-element.368), kind=kOutput, calls=%fused_computation.9.clone.1 | convolution fusion | flops 85862400 | bytes 3833920 | tf_op jit(solution)/shard_map/while/body/eval_jaxpr/bhqk,bkhe->bqhe/dot_general | solution.py:35
  211.8 1.8 pad_maximum_fusion.8
  219.1 3.0 %fusion.45 = (f32[16,129]{1,0:T(8,128)S(1)}, f32[16,129,320]{2,1,0:T(8,128)}) fusion(pred[320]{0:T(512)(128)(4,1)S(1)} %add_reduce_fusion.2, bf16[129,16,64]{0,2,1:T(8,128)(2,1)S(1)} %bitcast.78, bf16[320,16,64]{0,2,1:T(8,128)(2,1)S(1)} %bitcast.77), kind=kOutput, calls=%fused_computation.51.clone.1 | convolution fusion | flops 87183680 | bytes 3570048 | tf_op jit(solution)/shard_map/while/body/eval_jaxpr/sub | solution.py:33
  222.1 2.9 %fusion.46 = f32[16,64,129]{2,1,0:T(8,128)S(1)} fusion(bf16[320,16,64]{0,2,1:T(8,128)(2,1)S(1)} %bitcast.76, f32[16,129,320]{2,1,0:T(8,128)} %get-tuple-element.367, f32[16,129]{1,0:T(8,128)S(1)} %get-tuple-element.368), kind=kOutput, calls=%fused_computation.9.clone.1 | convolution fusion | flops 85862400 | bytes 3833920 | tf_op jit(solution)/shard_map/while/body/eval_jaxpr/bhqk,bkhe->bqhe/dot_general | solution.py:35
  230.0 1.8 pad_maximum_fusion.8
  237.3 3.0 %fusion.45 = (f32[16,129]{1,0:T(8,128)S(1)}, f32[16,129,320]{2,1,0:T(8,128)}) fusion(pred[320]{0:T(512)(128)(4,1)S(1)} %add_reduce_fusion.2, bf16[129,16,64]{0,2,1:T(8,128)(2,1)S(1)} %bitcast.78, bf16[320,16,64]{0,2,1:T(8,128)(2,1)S(1)} %bitcast.77), kind=kOutput, calls=%fused_computation.51.clone.1 | convolution fusion | flops 87183680 | bytes 3570048 | tf_op jit(solution)/shard_map/while/body/eval_jaxpr/sub | solution.py:33
  240.3 2.9 %fusion.46 = f32[16,64,129]{2,1,0:T(8,128)S(1)} fusion(bf16[320,16,64]{0,2,1:T(8,128)(2,1)S(1)} %bitcast.76, f32[16,129,320]{2,1,0:T(8,128)} %get-tuple-element.367, f32[16,129]{1,0:T(8,128)S(1)} %get-tuple-element.368), kind=kOutput, calls=%fused_computation.9.clone.1 | convolution fusion | flops 85862400 | bytes 3833920 | tf_op jit(solution)/shard_map/while/body/eval_jaxpr/bhqk,bkhe->bqhe/dot_general | solution.py:35
  244.9 3.1 %slice.51 = f32[4,1,128,1024]{2,3,1,0:T(8,128)} slice(f32[4,1,129,1024]{2,3,1,0:T(8,128)} %get-tuple-element.165), slice={[0:4], [0:1], [0:128], [0:1024]} | slice | bytes 4194304 | tf_op jit(solution)/shard_map/slice | solution.py:108
  248.0 3.7 %copy.57 = bf16[4,1,129,1024]{3,0,2,1:T(4,128)(2,1)S(1)} copy(f32[4,1,129,1024]{2,3,1,0:T(8,128)} %get-tuple-element.165) | data formatting | bytes 3170304 | tf_op jit(solution)/shard_map/while | solution.py:106
  251.7 1.9 copy.56
  (123 shorter events, 41.0 us)
Async XLA Ops:
  7.2 88.4 %all-gather.3.cloned.1.call-start = ((), (), s32[]{:S(2)}) async-start(), calls=%async_computation.1 | async-start | bytes 2621440 | tf_op jit(solution)/shard_map/all_gather | solution.py:70
  7.9 138.4 %all-gather.5.cloned.1.call-start = ((), (), s32[]{:S(2)}) async-start(), calls=%async_computation.2 | async-start | bytes 2621440 | tf_op jit(solution)/shard_map/all_gather | solution.py:69
  12.8 5.4 %copy-start.8 = (bf16[1,4,1024]{2,1,0:T(4,128)(2,1)S(1)}, bf16[1,4,1024]{2,1,0:T(4,128)(2,1)}, u32[]{:S(2)}) copy-start(bf16[1,4,1024]{2,1,0:T(4,128)(2,1)} %param.9) | copy-start | bytes 24580
  12.8 16.2 %copy-start.5 = (bf16[1,512,1024]{2,1,0:T(8,128)(2,1)S(1)}, bf16[1,512,1024]{2,1,0:T(8,128)(2,1)}, u32[]{:S(2)}) copy-start(bf16[1,512,1024]{2,1,0:T(8,128)(2,1)} %param.8) | copy-start | bytes 3145732
  12.8 141.1 %all-to-all-start = ((bf16[1024,4,256]{2,0,1:T(8,128)(2,1)}), bf16[1024,4,256]{2,0,1:T(8,128)(2,1)S(1)}, u32[]{:S(2)}, u32[]{:S(2)}) async-start(bf16[1024,4,256]{2,0,1:T(8,128)(2,1)} %copy.48), calls=%async_computation | async-start | bytes 4194304 | tf_op jit(solution)/shard_map/all_to_all | solution.py:13
  28.3 70.2 %copy-start.7 = (bf16[1,32,1024]{2,1,0:T(8,128)(2,1)}, bf16[1,32,1024]{2,1,0:T(8,128)(2,1)S(1)}, u32[]{:S(2)}) copy-start(bf16[1,32,1024]{2,1,0:T(8,128)(2,1)S(1)} %copy.43) | copy-start | bytes 196612
  29.3 69.2 %copy-start.9 = (bf16[1,4,1024]{2,1,0:T(4,128)(2,1)}, bf16[1,4,1024]{2,1,0:T(4,128)(2,1)S(1)}, u32[]{:S(2)}) copy-start(bf16[1,4,1024]{2,1,0:T(4,128)(2,1)S(1)} %fusion.20) | copy-start | bytes 24580
  98.5 1.1 copy-start.3
  100.2 66.2 %collective-permute-start.1 = (bf16[1,32,1024]{2,1,0:T(8,128)(2,1)}, bf16[1,32,1024]{2,1,0:T(8,128)(2,1)}, u32[]{:S(2)}, u32[]{:S(2)}) collective-permute-start(bf16[1,32,1024]{2,1,0:T(8,128)(2,1)} %get-tuple-element.281), channel_id=1, source_target_pairs={{1,0},{2,1},{3,2},{4,3},{5,4},{6,5},{7,6},{9,8},{10,9},{11,10},{12... | collective-permute-start | bytes 196616 | tf_op jit(solution)/shard_map/ppermute | solution.py:19
  102.6 63.8 %collective-permute-start = (bf16[1,128,1024]{2,1,0:T(8,128)(2,1)S(1)}, bf16[1,128,1024]{2,1,0:T(8,128)(2,1)}, u32[]{:S(2)}, u32[]{:S(2)}) collective-permute-start(bf16[1,128,1024]{2,1,0:T(8,128)(2,1)S(1)} %slice.53), channel_id=1, source_target_pairs={{0,1},{1,2},{2,3},{3,4},{4,5},{5,6},{6,7},{8,9},{9,10},{10,11},{11... | collective-permute-start | bytes 786440 | tf_op jit(solution)/shard_map/ppermute | solution.py:19
  149.6 12.0 %copy-start.2 = (bf16[1,548,1024]{2,1,0:T(8,128)(2,1)}, bf16[1,548,1024]{2,1,0:T(8,128)(2,1)S(1)}, u32[]{:S(2)}) copy-start(bf16[1,548,1024]{2,1,0:T(8,128)(2,1)S(1)} %fusion.17) | copy-start | bytes 3366916
  150.3 19.6 %collective-permute-start.2 = (bf16[1,128,1024]{2,1,0:T(8,128)(2,1)}, bf16[1,128,1024]{2,1,0:T(8,128)(2,1)}, u32[]{:S(2)}, u32[]{:S(2)}) collective-permute-start(bf16[1,128,1024]{2,1,0:T(8,128)(2,1)} %slice.59), channel_id=1, source_target_pairs={{0,1},{1,2},{2,3},{3,4},{4,5},{5,6},{6,7},{8,9},{9,10},{10,11},{11... | collective-permute-start | bytes 786440 | tf_op jit(solution)/shard_map/ppermute | solution.py:19
  156.5 4.1 %copy-start.4 = (bf16[1,548,1024]{2,1,0:T(8,128)(2,1)S(1)}, bf16[1,548,1024]{2,1,0:T(8,128)(2,1)}, u32[]{:S(2)}) copy-start(bf16[1,548,1024]{2,1,0:T(8,128)(2,1)} %copy-done.3) | copy-start | bytes 3366916
  162.6 7.3 %slice-start = ((bf16[1,548,1024]{2,1,0:T(8,128)(2,1)}), bf16[1,512,1024]{2,1,0:T(8,128)(2,1)S(1)}, s32[]{:S(2)}) async-start(bf16[1,548,1024]{2,1,0:T(8,128)(2,1)} %copy-done.2), calls=%async_computation.3 | async-start | bytes 2097152 | tf_op jit(solution)/shard_map/slice | solution.py:78
  163.2 6.7 %collective-permute-start.3 = (bf16[1,32,1024]{2,1,0:T(8,128)(2,1)}, bf16[1,32,1024]{2,1,0:T(8,128)(2,1)S(1)}, u32[]{:S(2)}, u32[]{:S(2)}) collective-permute-start(bf16[1,32,1024]{2,1,0:T(8,128)(2,1)} %get-tuple-element.279), channel_id=1, source_target_pairs={{1,0},{2,1},{3,2},{4,3},{5,4},{6,5},{7,6},{9,8},{10,9},{11,10},{12... | collective-permute-start | bytes 196616 | tf_op jit(solution)/shard_map/ppermute | solution.py:19
  166.4 5.8 %copy-start.6 = (bf16[1,4,1024]{2,1,0:T(4,128)(2,1)S(1)}, bf16[1,4,1024]{2,1,0:T(4,128)(2,1)}, u32[]{:S(2)}) copy-start(bf16[1,4,1024]{2,1,0:T(4,128)(2,1)} %slice.58) | copy-start | bytes 24580
  172.1 1.8 copy-start
  188.6 1.7 copy-start.1
  190.3 1.8 copy-start
  206.8 1.7 copy-start.1
  208.5 1.8 copy-start
  225.0 1.7 copy-start.1
  226.7 1.8 copy-start
  243.2 1.7 copy-start.1
  251.7 2.5 copy-start.10
Sparse Core Ops, SparseCore 0:
  9.5 85.9 all-gather.2
  97.1 49.1 all-gather.4
